TPU v7x, 128 devices: a whole 4x4x4 slice. The times are simulated.
128 devices in a mesh: ens: 8 (over y_lo, z), rep: 16 (over y_hi, x, core).
Axes of the slice: x: 4, y: 4 (y_hi: 2, y_lo: 2; y = y_hi * 2 + y_lo), z: 4, core: 2. Of those that a mesh axis runs over, the one named last changes fastest.
Arguments:
- cur_states: bfloat16 [32768, 4096], P('rep'), may hold values from -6 to 6
- buffer: bfloat16 [4096, 4096], P('rep'), may hold values from -6 to 6
- fetch_rows: int32 [16, 16, 128], P('rep'), may hold values from 0 to 255
- fetch_counts: int32 [16, 16], replicated, may hold values from 1 to 128, as said below
- actions: int32 [32768], P('rep'), may hold values from 0 to 255
- rewards: float32 [32768], P('rep'), may hold values from -0.5 to 0.5
- terminal: int32 [32768], P('rep'), may hold values 0 or 1
- mc_return: float32 [32768], P('rep'), may hold values from 0 to 1
- w_in: bfloat16 [8, 4096, 512], P('ens'), may hold values from -0.09375 to 0.09375
- w_out: bfloat16 [8, 512, 256], P('ens'), may hold values from -0.25 to 0.25
Outputs:
- targets: float32 [32768], P('rep')
- grad_in: float32 [8, 4096, 512], P('ens', 'rep')
- grad_out: float32 [8, 512, 256], P('ens', 'rep')
Inputs may be any that keep to these rules, and one draw needn't show every extreme that they name: `fetch_rows`: each entry indexes the owner's own rows. `fetch_counts`: entry [o, r] is how many leading slots of requester r at owner o are used; some entry equals 128 in every draw.
All inputs are finite; a program needn't handle non-finite values. No bound on the sum of `terminal` on one device may be relied on, other than what follows from the above.
Results may differ from a plain program's by a relative error of at most 0.0044.
Values may be sent and summed in bfloat16 or wider, within the bound.
No kernel may reach another device: no remote copies, remote signals or barrier semaphores. Data moves between devices by JAX's collectives and lax.ppermute only.
A program may use at most 192 MiB of HBM per device.

v0:
```python
import jax
import jax.numpy as jnp
from jax import lax
from jax.sharding import PartitionSpec as P


def sent_to_all(shard, axis):
    count = lax.axis_size(axis)
    return lax.all_to_all(
        jnp.broadcast_to(shard[None], (count, *shard.shape)), axis, 0, 0, tiled=True
    )


def taken_together(shard, axis):
    return sent_to_all(shard, axis).min(axis=0)


def split_up(shard, dim, count):
    shape = shard.shape
    blocks = shard.reshape(*shape[:dim], count, shape[dim] // count, *shape[dim + 1 :])
    return jnp.moveaxis(blocks, dim, 0)


def one_scatter(arrays, axis, dims):
    count = lax.axis_size(axis)
    blocks = [split_up(a, dim, count) for a, dim in zip(arrays, dims)]
    lines = jnp.concatenate([b.reshape(count, -1) for b in blocks], axis=1)
    rows = max(16, -(-lines.shape[1] // 1024) * 8)
    lines = jnp.pad(lines, ((0, 0), (0, rows * 128 - lines.shape[1]))).reshape(-1, 128)
    flat, at, gathered = (lax.psum_scatter(lines, axis, tiled=True).reshape(-1), 0, [])
    for b in blocks:
        part = b[0]
        gathered.append(flat[at : at + part.size].reshape(part.shape))
        at += part.size
    return tuple(gathered)


def critic_head(features, w_first, w_second):
    preact = jnp.dot(features, w_first, preferred_element_type=jnp.float32)
    sigmoid_pre = jax.nn.sigmoid(preact)
    hidden = (preact * sigmoid_pre).astype(jnp.bfloat16)
    values = jax.nn.sigmoid(jnp.dot(hidden, w_second, preferred_element_type=jnp.float32))
    return (preact, sigmoid_pre, hidden, values)


def shards(
    cur_states, buffer, fetch_rows, fetch_counts, actions, rewards, terminal, mc_return, w_in, w_out
):
    my_index = lax.axis_index("rep")
    owners = lax.axis_size("rep")
    slots_per = fetch_rows.shape[2]
    width = buffer.shape[1]
    w_first = w_in[0]
    w_second = w_out[0]
    my_counts = lax.dynamic_slice_in_dim(fetch_counts, my_index, 1, 1)[:, 0]
    slot_ids = jnp.arange(slots_per, dtype=jnp.int32)
    used = (slot_ids[None, :] < my_counts[:, None]).reshape(-1).astype(jnp.float32)
    counted = jnp.sum(fetch_counts).astype(jnp.float32)
    picked = jnp.take(buffer, fetch_rows[0].reshape(-1), axis=0).reshape(owners, slots_per, width)
    values = critic_head(picked.reshape(-1, width), w_first, w_second)[3]
    served = jnp.max(values, axis=1).reshape(picked.shape[0], picked.shape[1])
    best_next = lax.all_to_all(served, "rep", split_axis=0, concat_axis=0, tiled=True).reshape(-1)
    ens_floor = taken_together(best_next, "ens")
    bootstrap = jnp.maximum(ens_floor, mc_return)
    target = rewards + 0.98 * (1.0 - terminal.astype(jnp.float32)) * bootstrap
    targets = used * target
    chosen = actions[:, None] == jnp.arange(w_second.shape[1], dtype=jnp.int32)[None, :]
    preact, sigmoid_pre, hidden, values = critic_head(cur_states, w_first, w_second)
    taken = jnp.sum(jnp.where(chosen, values, 0.0), axis=1)
    errors = used * 2.0 * (taken - target) * taken * (1.0 - taken) * (65536.0 / counted)
    d_logits = jnp.where(chosen, errors[:, None], 0.0).astype(jnp.bfloat16)
    grad_second = lax.dot_general(
        hidden, d_logits, (((0,), (0,)), ((), ())), preferred_element_type=jnp.float32
    )
    back = lax.dot_general(
        d_logits, w_second, (((1,), (1,)), ((), ())), preferred_element_type=jnp.float32
    )
    d_hidden = (back * sigmoid_pre * (1.0 + preact * (1.0 - sigmoid_pre))).astype(jnp.bfloat16)
    grad_first = lax.dot_general(
        cur_states, d_hidden, (((0,), (0,)), ((), ())), preferred_element_type=jnp.float32
    )
    share_first, share_second = one_scatter((grad_first, grad_second), "rep", (0, 0))
    return (targets, share_first[None], share_second[None])


def solution(mesh):
    placed = (
        P("rep", None),
        P("rep", None),
        P("rep", None, None),
        P(),
        P("rep"),
        P("rep"),
        P("rep"),
        P("rep"),
        P("ens", None, None),
        P("ens", None, None),
    )
    return jax.shard_map(
        shards,
        mesh=mesh,
        in_specs=placed,
        out_specs=(P("rep"), P("ens", "rep", None), P("ens", "rep", None)),
        check_vma=False,
    )
```

profile of v0, /device:TPU:0, one launch (start us, length us, event | category | flops | bytes accessed | tf_op | source)
XLA Modules:
  0.0 243.3 jit_solution(17041579490069059682)
XLA Ops:
  7.2 0.0 copy-start
  7.2 0.9 compare_and_fusion
  8.0 0.7 compare_select_fusion
  8.8 0.0 copy-done
  8.8 0.0 copy-start.6
  8.8 14.3 %gather_fusion = bf16[2048,4096]{1,0:T(8,128)(2,1)} fusion(bf16[256,4096]{1,0:T(8,128)(2,1)S(1)} %copy-done, s32[2048]{0:T(1024)S(1)} %broadcast_clamp_fusion), kind=kCustom, calls=%fused_computation | custom fusion | bytes 33562624 | tf_op jit(solution)/shard_map/jit(_take)/gather | solution.py:59
  23.1 0.0 copy-done.6
  23.1 15.6 %fusion.23 = f32[2048]{0:T(1024)} fusion(bf16[1,4096,512]{2,1,0:T(8,128)(2,1)} %param.18, bf16[2048,4096]{1,0:T(8,128)(2,1)} %gather_fusion, pred[2048]{0:T(1024)(128)(4,1)S(1)} %compare_and_fusion, bf16[1,512,256]{2,1,0:T(8,128)(2,1)S(1)} %copy-done.6), kind=kOutput, calls=%fused_computation.26 | convolution fusion | flops 9142532096 | bytes 21243904 | tf_op jit(solution)/shard_map/dot_general | solution.py:42
  38.7 7.2 %all-to-all-start = ((f32[16,1,128]{2,1,0:T(1,128)}), f32[16,1,128]{2,1,0:T(1,128)S(1)}, u32[]{:S(2)}, u32[]{:S(2)}) async-start(f32[16,1,128]{2,1,0:T(1,128)} %bitcast.6), calls=%async_computation | async-start | bytes 16384 | tf_op jit(solution)/shard_map/all_to_all | solution.py:62
  45.9 0.0 copy-start.7
  45.9 15.7 %multiply_convert_fusion.1 = (bf16[2048,512]{1,0:T(8,128)(2,1)}, f32[2048,512]{1,0:T(8,128)}) fusion(bf16[2048,4096]{1,0:T(8,128)(2,1)} %param.10, bf16[1,4096,512]{2,1,0:T(8,128)(2,1)} %param.18), kind=kOutput, calls=%fused_computation.11 | convolution fusion | flops 8595177472 | bytes 27262976 | tf_op jit(solution)/shard_map/dot_general | solution.py:39
  61.6 0.0 all-to-all-done
  61.6 0.7 broadcast_in_dim.38
  62.3 5.4 %all-to-all-start.1 = ((f32[8,1,2048]{2,1,0:T(1,128)}), f32[8,1,2048]{2,1,0:T(1,128)S(1)}, u32[]{:S(2)}, u32[]{:S(2)}) async-start(f32[8,1,2048]{2,1,0:T(1,128)} %broadcast_in_dim.38), calls=%async_computation.1 | async-start | bytes 131072 | tf_op jit(solution)/shard_map/all_to_all | solution.py:9
  67.7 0.2 reduce-scatter.2.cloned.1.call-start
  67.9 0.0 copy-done.7
  68.0 0.0 copy-start.2
  68.0 0.0 copy-start.3
  68.0 0.0 copy-start.4
  68.0 0.0 copy-start.5
  68.0 2.7 %fusion.28 = f32[2048]{0:T(1024)S(1)} fusion(bf16[2048,512]{1,0:T(8,128)(2,1)} %get-tuple-element.5, s32[2048]{0:T(1024)S(1)} %copy-done.7, bf16[1,512,256]{2,1,0:T(8,128)(2,1)S(1)} %copy-done.6), kind=kOutput, calls=%fused_computation.27 | convolution fusion | flops 540014592 | bytes 2375680 | tf_op jit(solution)/shard_map/dot_general | solution.py:42
  70.7 0.0 copy-done.2
  70.7 0.6 reduce_sum.19
  72.1 0.2 dynamic-slice_reduce_fusion
  72.2 1.8 all-to-all-done.1
  74.1 0.1 reduce_min.9
  74.1 0.0 copy-done.3
  74.1 0.0 copy-done.4
  74.1 0.0 copy-done.5
  74.2 0.1 multiply_multiply_fusion
  74.2 2.3 fusion.22
  76.6 0.1 reshape_reshape.7
  76.7 19.0 %convolution_bitcast_fusion = f32[4096,512]{0,1:T(8,128)} fusion(bf16[2048,4096]{1,0:T(8,128)(2,1)} %param.10, f32[2048,512]{1,0:T(8,128)} %get-tuple-element.6, bf16[2048]{0:T(1024)(128)(2,1)S(1)} %get-tuple-element.3, s32[2048]{0:T(1024)S(1)} %copy-done.7, bf16[1,512,256]{2,1,0:T(8,128)(2,1)S(1)} %copy-done.6), kind=kOutput, calls=%fused_computation.6 | convolution fusion | flops 9137291264 | bytes 29634560 | tf_op jit(solution)/shard_map/dot_general | solution.py:79
  95.7 9.0 %copy.16 = f32[4096,512]{1,0:T(8,128)} copy(f32[4096,512]{0,1:T(8,128)} %convolution_bitcast_fusion) | data formatting | bytes 16777216 | tf_op jit(solution)/shard_map/dot_general | solution.py:79
  104.7 6.2 %reshape_reshape.6 = f32[16,131072]{1,0:T(8,128)} reshape(f32[4096,512]{1,0:T(8,128)} %copy.16) | data formatting | bytes 16777216 | tf_op jit(solution)/shard_map/reshape;reshape | solution.py:27
  110.9 6.4 %pad_maximum_fusion = f32[16,139264]{1,0:T(8,128)} fusion(f32[16,8192]{1,0:T(8,128)S(1)} %reshape_reshape.7, f32[16,131072]{1,0:T(8,128)} %reshape_reshape.6), kind=kLoop, calls=%fused_computation.4 | loop fusion | flops 2228224 | bytes 17825792 | tf_op jit(solution)/shard_map/concatenate | solution.py:27
  117.3 10.0 %reshape.67 = f32[17408,128]{1,0:T(8,128)} reshape(f32[16,139264]{1,0:T(8,128)} %pad_maximum_fusion) | data formatting | bytes 17825792 | tf_op jit(solution)/shard_map/reshape | solution.py:29
  127.3 0.0 copy-start.1
  127.3 0.0 reduce-scatter.2.cloned.1.call-update
  127.3 0.7 fusion.43
  128.0 105.1 %reduce-scatter.2.cloned.1.call-done = f32[1088,128]{1,0:T(8,128)} async-done(((f32[17408,128]{1,0:T(8,128)}), f32[1088,128]{1,0:T(8,128)}) %reduce-scatter.2.cloned.1.call-update) | async-done | bytes 557072 | tf_op jit(solution)/shard_map/reduce_scatter | solution.py:30
  233.1 1.1 slice.12
  234.2 0.9 broadcast_in_dim_reshape.7
  235.0 0.8 slice.13
  235.8 0.6 broadcast_in_dim_reshape.8
  236.4 0.0 copy-done.1
  (1 shorter events, 0.0 us)
Async XLA Ops:
  7.2 1.6 copy-start
  8.8 14.3 %copy-start.6 = (bf16[1,512,256]{2,1,0:T(8,128)(2,1)S(1)}, bf16[1,512,256]{2,1,0:T(8,128)(2,1)}, u32[]{:S(2)}) copy-start(bf16[1,512,256]{2,1,0:T(8,128)(2,1)} %param.19) | copy-start | bytes 786436
  38.7 22.9 %all-to-all-start = ((f32[16,1,128]{2,1,0:T(1,128)}), f32[16,1,128]{2,1,0:T(1,128)S(1)}, u32[]{:S(2)}, u32[]{:S(2)}) async-start(f32[16,1,128]{2,1,0:T(1,128)} %bitcast.6), calls=%async_computation | async-start | bytes 16384 | tf_op jit(solution)/shard_map/all_to_all | solution.py:62
  45.9 22.1 %copy-start.7 = (s32[2048]{0:T(1024)S(1)}, s32[2048]{0:T(1024)}, u32[]{:S(2)}) copy-start(s32[2048]{0:T(1024)} %param.14) | copy-start | bytes 24580
  62.3 11.8 %all-to-all-start.1 = ((f32[8,1,2048]{2,1,0:T(1,128)}), f32[8,1,2048]{2,1,0:T(1,128)S(1)}, u32[]{:S(2)}, u32[]{:S(2)}) async-start(f32[8,1,2048]{2,1,0:T(1,128)} %broadcast_in_dim.38), calls=%async_computation.1 | async-start | bytes 131072 | tf_op jit(solution)/shard_map/all_to_all | solution.py:9
  67.7 165.4 %reduce-scatter.2.cloned.1.call-start = ((), (), s32[]{:S(2)}) async-start(), calls=%async_computation.3 | async-start | bytes 9469952 | tf_op jit(solution)/shard_map/reduce_scatter | solution.py:30
  68.0 2.8 %copy-start.2 = (s32[16,16]{1,0:T(8,128)S(1)}, s32[16,16]{1,0:T(8,128)}, u32[]{:S(2)}) copy-start(s32[16,16]{1,0:T(8,128)} %param.13) | copy-start | bytes 3076
  68.0 6.2 %copy-start.3 = (f32[2048]{0:T(1024)S(1)}, f32[2048]{0:T(1024)}, u32[]{:S(2)}) copy-start(f32[2048]{0:T(1024)} %param.15) | copy-start | bytes 24580
  68.0 6.2 %copy-start.4 = (f32[2048]{0:T(1024)S(1)}, f32[2048]{0:T(1024)}, u32[]{:S(2)}) copy-start(f32[2048]{0:T(1024)} %param.17) | copy-start | bytes 24580
  68.0 6.2 %copy-start.5 = (s32[2048]{0:T(1024)S(1)}, s32[2048]{0:T(1024)}, u32[]{:S(2)}) copy-start(s32[2048]{0:T(1024)} %param.16) | copy-start | bytes 24580
  127.3 109.1 %copy-start.1 = (bf16[256,4096]{1,0:T(8,128)(2,1)S(1)}, bf16[256,4096]{1,0:T(8,128)(2,1)}, u32[]{:S(2)}) copy-start(bf16[256,4096]{1,0:T(8,128)(2,1)} %param.11) | copy-start | bytes 6291460
Sparse Core Ops, SparseCore 0:
  127.4 105.5 reduce-scatter.1
where the time goes:
time: 244 us; the launch traced here: 243 us
  waiting for transfers between devices  107 us (44%)
  matrix products  55.4 us (23%)
  local copies, waits for them, and re-layouts  43.8 us (18%)
  between operations  14.9 us (6%)
  starting transfers between devices  12.8 us (5%)
  other arithmetic  9.44 us (4%)
    reduce_scatter x1, waiting for transfers between devices, one_scatter(): lax.psum_scatter(lines, axis, tiled=True).reshape(-1)  105 us
    dot_general x1, matrix products, shards(): lax.dot_general(cur_states, d_hidden, (((0,), (0,)), ((), ())), preferred...  19 us
    dot_general x2, matrix products, critic_head(): jnp.dot(hidden, w_second, preferred_element_type=jnp.float32)  18.3 us
    dot_general x1, matrix products, critic_head(): preact = jnp.dot(features, w_first, preferred_element_type=jnp.float32)  15.7 us
    gather x1, local copies, waits for them, and re-layouts, shards(): jnp.take(buffer, fetch_rows[0].reshape(-1), axis=0)  14.3 us
    reshape x1, local copies, waits for them, and re-layouts, one_scatter(): jnp.pad(lines, ((0, 0), (0, rows * 128 - lines.shape[1]))).reshape(-1, 128)  9.96 us
    dot_general x1, local copies, waits for them, and re-layouts, shards(): lax.dot_general(cur_states, d_hidden, (((0,), (0,)), ((), ())), preferred...  8.99 us
    all_to_all x1, starting transfers between devices, shards(): lax.all_to_all(served, 'rep', split_axis=0, concat_axis=0, tiled=True)  7.15 us
  transfers between devices with their start and end apart: 3, of which 2 were waited for; matrix products, arithmetic and copies ran while one was open for 8% of the time, Pallas kernels for 0%

commit v1 on v0

v1 whole, which is shorter than its diff:
```python
import jax
import jax.numpy as jnp
from jax import lax
from jax.sharding import PartitionSpec as P


def place(y, x, core):
    return y * 8 + x * 2 + core


def moves(fn):
    return [
        (place(y, x, c), place(*fn(y, x, c)))
        for y in range(2)
        for x in range(4)
        for c in range(2)
    ]


CORE = moves(lambda y, x, c: (y, x, 1 - c))
RIGHT = moves(lambda y, x, c: (y, (x + 1) % 4, c))
LEFT = moves(lambda y, x, c: (y, (x + 3) % 4, c))
ACROSS = moves(lambda y, x, c: (1 - y, x, c))


def sent(value, pairs):
    return lax.ppermute(value, "rep", pairs)


def low(value):
    return value.astype(jnp.bfloat16)


def high(value):
    return value.astype(jnp.float32)


def reduced(piece, y, x, core):
    far, right, left = (x + 2) & 3, (x + 1) & 3, (x + 3) & 3
    other, same = 1 - y, y
    partner = 1 - core

    def pair(x_at):
        away = sent(jnp.stack([low(piece(h, x_at, partner)) for h in (other, same)]), CORE)
        kept = [piece(h, x_at, core) for h in (other, same)]
        return [k + high(away[i]) for i, k in enumerate(kept)]

    far_other, far_same = pair(far)
    from_left_far = sent(low(far_other), RIGHT)
    from_right_far = sent(low(far_same), LEFT)
    right_other, right_same = pair(right)
    left_other, left_same = pair(left)
    from_left_same = sent(low(right_same), RIGHT)
    from_right_other = sent(low(left_other), LEFT)
    from_left_other = sent(low(right_other + high(from_left_far)), RIGHT)
    from_right_same = sent(low(left_same + high(from_right_far)), LEFT)
    own_other, own_same = pair(x)
    own_other = own_other + high(from_right_other) + high(from_left_other)
    over = sent(low(own_other), ACROSS)
    own_same = own_same + high(from_left_same) + high(from_right_same)
    return own_same + high(over)


def sent_to_all(shard, axis):
    count = lax.axis_size(axis)
    return lax.all_to_all(
        jnp.broadcast_to(shard[None], (count, *shard.shape)), axis, 0, 0, tiled=True
    )


def critic_head(features, w_first, w_second):
    preact = jnp.dot(features, w_first, preferred_element_type=jnp.float32)
    sigmoid_pre = jax.nn.sigmoid(preact)
    hidden = (preact * sigmoid_pre).astype(jnp.bfloat16)
    logits = jnp.dot(hidden, w_second, preferred_element_type=jnp.float32)
    return (preact, sigmoid_pre, hidden, logits)


def shards(
    cur_states, buffer, fetch_rows, fetch_counts, actions, rewards, terminal, mc_return, w_in, w_out
):
    my_index = lax.axis_index("rep").astype(jnp.uint32)
    core, x, y = my_index & 1, (my_index >> 1) & 3, my_index >> 3
    slots_per = fetch_rows.shape[2]
    w_first = w_in[0]
    w_second = w_out[0]
    my_counts = lax.dynamic_slice_in_dim(fetch_counts, my_index, 1, 1)[:, 0]
    slot_ids = jnp.arange(slots_per, dtype=jnp.int32)
    used = (slot_ids[None, :] < my_counts[:, None]).reshape(-1).astype(jnp.float32)
    counted = jnp.sum(fetch_counts).astype(jnp.float32)

    row_best = jax.nn.sigmoid(jnp.max(critic_head(buffer, w_first, w_second)[3], axis=1))
    row_floor = sent_to_all(row_best, "ens").min(axis=0)
    row_ids = jnp.arange(buffer.shape[0], dtype=jnp.int32)
    served = jnp.sum(
        jnp.where(fetch_rows[0][:, :, None] == row_ids[None, None, :], row_floor, 0.0), axis=2
    )
    ens_floor = lax.all_to_all(served, "rep", split_axis=0, concat_axis=0, tiled=True).reshape(-1)

    bootstrap = jnp.maximum(ens_floor, mc_return)
    target = rewards + 0.98 * (1.0 - terminal.astype(jnp.float32)) * bootstrap
    targets = used * target
    chosen = actions[:, None] == jnp.arange(w_second.shape[1], dtype=jnp.int32)[None, :]
    preact, sigmoid_pre, hidden, logits = critic_head(cur_states, w_first, w_second)
    taken = jax.nn.sigmoid(jnp.sum(jnp.where(chosen, logits, 0.0), axis=1))
    errors = used * 2.0 * (taken - target) * taken * (1.0 - taken) * (65536.0 / counted)
    d_logits = jnp.where(chosen, errors[:, None], 0.0).astype(jnp.bfloat16)
    grad_second = lax.dot_general(
        hidden, d_logits, (((0,), (0,)), ((), ())), preferred_element_type=jnp.float32
    )
    back = lax.dot_general(
        d_logits, w_second, (((1,), (1,)), ((), ())), preferred_element_type=jnp.float32
    )
    d_hidden = (back * sigmoid_pre * (1.0 + preact * (1.0 - sigmoid_pre))).astype(jnp.bfloat16)
    d_hidden = lax.optimization_barrier(d_hidden)

    depth = cur_states.shape[1] // 16
    rows_second = grad_second.shape[0] // 16

    def piece(y_at, x_at, core_at):
        at = place(y_at, x_at, core_at)
        columns = lax.dynamic_slice_in_dim(cur_states, at * depth, depth, 1)
        first = lax.dot_general(
            d_hidden, columns, (((0,), (0,)), ((), ())), preferred_element_type=jnp.float32
        )
        second = lax.dynamic_slice_in_dim(grad_second, at * rows_second, rows_second, 0)
        return jnp.concatenate([first, second])

    share = reduced(piece, y, x, core)
    width = w_first.shape[1]
    return (targets, share[:width].T[None], share[width:][None])


def solution(mesh):
    placed = (
        P("rep", None),
        P("rep", None),
        P("rep", None, None),
        P(),
        P("rep"),
        P("rep"),
        P("rep"),
        P("rep"),
        P("ens", None, None),
        P("ens", None, None),
    )
    return jax.shard_map(
        shards,
        mesh=mesh,
        in_specs=placed,
        out_specs=(P("rep"), P("ens", "rep", None), P("ens", "rep", None)),
        check_vma=False,
    )
```

time: 244 us -> 98.3 us (0.40)
  waiting for transfers between devices: 107 us -> 21.4 us
  local copies, waits for them, and re-layouts: 43.8 us -> 5.67 us
  matrix products: 55.4 us -> 41 us
  between operations: 14.9 us -> 1.74 us
  starting transfers between devices: 12.8 us -> 24.4 us
  other arithmetic: 9.44 us -> 3.79 us
    reduce_scatter x1 -> x0, waiting for transfers between devices: 105 us -> none  [one_scatter(): lax.psum_scatter(lines, axis, tiled=True).reshape(-1)]
    ppermute x0 -> x11, waiting for transfers between devices: none -> 17.9 us  [sent(): return lax.ppermute(value, 'rep', pairs)]
    dot_general x3 -> x19, matrix products: 37.4 us -> 22.7 us  [the longest x16 12.3 us: piece(): lax.dot_general(d_hidden, columns, (((0,), (0,)), ((), ())), preferred_el...]
    gather x1 -> x0, local copies, waits for them, and re-layouts: 14.3 us -> none  [shards(): jnp.take(buffer, fetch_rows[0].reshape(-1), axis=0)]
    ppermute x0 -> x11, starting transfers between devices: none -> 11.2 us  [sent(): return lax.ppermute(value, 'rep', pairs)]
    reshape x1 -> x0, local copies, waits for them, and re-layouts: 9.96 us -> none  [one_scatter(): jnp.pad(lines, ((0, 0), (0, rows * 128 - lines.shape[1]))).reshape(-1, 128)]
    dot_general x1 -> x0, local copies, waits for them, and re-layouts: 8.99 us -> none  [shards(): lax.dot_general(cur_states, d_hidden, (((0,), (0,)), ((), ())), preferred...]
    another operation x4 -> x0, local copies, waits for them, and re-layouts: 7.78 us -> none  [the longest x2 6.28 us: one_scatter(): lines = jnp.concatenate([b.reshape(count, -1) for b in blocks], axis=1)]
  transfers between devices with their start and end apart: 3 -> 13, of which waited for: 2 -> 7; matrix products, arithmetic and copies ran while one was open for 8% -> 32% of each run, Pallas kernels for 0% -> 0%
where the time goes in v1:
time: 98.3 us; the launch traced here: 98 us
  matrix products  41 us (42%)
  starting transfers between devices  24.4 us (25%)
  waiting for transfers between devices  21.4 us (22%)
  local copies, waits for them, and re-layouts  5.67 us (6%)
  other arithmetic  3.79 us (4%)
  between operations  1.74 us (2%)
    ppermute x11, waiting for transfers between devices, sent(): return lax.ppermute(value, 'rep', pairs)  17.9 us
    dot_general x1, matrix products, critic_head(): preact = jnp.dot(features, w_first, preferred_element_type=jnp.float32)  15.8 us
    dot_general x16, matrix products, piece(): lax.dot_general(d_hidden, columns, (((0,), (0,)), ((), ())), preferred_el...  12.3 us
    ppermute x11, starting transfers between devices, sent(): return lax.ppermute(value, 'rep', pairs)  11.2 us
    all_to_all x1, starting transfers between devices, shards(): lax.all_to_all(served, 'rep', split_axis=0, concat_axis=0, tiled=True)  6.75 us
    all_to_all x1, starting transfers between devices, sent_to_all(): lax.all_to_all(jnp.broadcast_to(shard[None], (count, *shard.shape)), axis...  6.44 us
    dot_general x2, matrix products, critic_head(): logits = jnp.dot(hidden, w_second, preferred_element_type=jnp.float32)  6.11 us
    dot_general x1, matrix products, shards(): lax.dot_general(d_logits, w_second, (((1,), (1,)), ((), ())), preferred_e...  4.33 us
  transfers between devices with their start and end apart: 13, of which 7 were waited for; matrix products, arithmetic and copies ran while one was open for 32% of the time, Pallas kernels for 0%

profile of v1, /device:TPU:0, one launch (start us, length us, event | category | flops | bytes accessed | tf_op | source)
XLA Modules:
  0.0 98.0 jit_solution(847345825016676419)
XLA Ops:
  0.6 1.6 %copy-done = bf16[256,4096]{1,0:T(8,128)(2,1)S(1)} copy-done((bf16[256,4096]{1,0:T(8,128)(2,1)S(1)}, bf16[256,4096]{1,0:T(8,128)(2,1)}, u32[]{:S(2)}) %copy-start) | copy-done | bytes 2097176
  2.2 3.7 %convolution_reduce_fusion = f32[256]{0:T(256)S(1)} fusion(bf16[256,4096]{1,0:T(8,128)(2,1)S(1)} %copy-done, bf16[1,4096,512]{2,1,0:T(8,128)(2,1)} %param.18, bf16[1,512,256]{2,1,0:T(8,128)(2,1)} %param.19), kind=kOutput, calls=%fused_computation.30 | convolution fusion | flops 1141571328 | bytes 6554624 | tf_op jit(solution)/shard_map/dot_general | solution.py:75
  6.0 0.6 broadcast_in_dim.39
  6.6 6.4 %all-to-all-start = ((f32[8,1,256]{2,1,0:T(1,128)}), f32[8,1,256]{2,1,0:T(1,128)S(1)}, u32[]{:S(2)}, u32[]{:S(2)}) async-start(f32[8,1,256]{2,1,0:T(1,128)} %broadcast_in_dim.39), calls=%async_computation | async-start | bytes 16384 | tf_op jit(solution)/shard_map/all_to_all | solution.py:66
  13.1 15.8 %multiply_convert_fusion.1 = (bf16[2048,512]{1,0:T(8,128)(2,1)}, f32[2048,512]{1,0:T(8,128)}) fusion(bf16[2048,4096]{1,0:T(8,128)(2,1)} %param.10, bf16[1,4096,512]{2,1,0:T(8,128)(2,1)} %param.18), kind=kOutput, calls=%fused_computation.5 | convolution fusion | flops 8595177472 | bytes 27262976 | tf_op jit(solution)/shard_map/dot_general | solution.py:72
  28.9 1.4 %select_reduce_fusion = f32[16,128]{1,0:T(8,128)} fusion(f32[256]{0:T(256)S(1)} %reduce_min.9, s32[16,128]{1,0:T(8,128)S(1)} %bitcast.130), kind=kLoop, calls=%fused_computation.10 | loop fusion | flops 1570816 | bytes 17408 | tf_op jit(solution)/shard_map/reduce_sum | solution.py:95
  30.3 6.7 %all-to-all-start.1 = ((f32[16,1,128]{2,1,0:T(1,128)}), f32[16,1,128]{2,1,0:T(1,128)S(1)}, u32[]{:S(2)}, u32[]{:S(2)}) async-start(f32[16,1,128]{2,1,0:T(1,128)} %bitcast.5), calls=%async_computation.1 | async-start | bytes 16384 | tf_op jit(solution)/shard_map/all_to_all | solution.py:98
  37.1 2.4 %fusion.4 = f32[2048]{0:T(1024)S(1)} fusion(bf16[2048,512]{1,0:T(8,128)(2,1)} %get-tuple-element.42, s32[2048]{0:T(1024)S(1)} %copy-done.7, bf16[1,512,256]{2,1,0:T(8,128)(2,1)S(1)} %copy-done.6), kind=kOutput, calls=%fused_computation.12 | convolution fusion | flops 538441728 | bytes 2375680 | tf_op jit(solution)/shard_map/dot_general | solution.py:75
  39.5 0.6 reduce_sum.29
  41.0 3.5 %all-to-all-done.1 = f32[16,1,128]{2,1,0:T(1,128)S(1)} async-done(((f32[16,1,128]{2,1,0:T(1,128)}), f32[16,1,128]{2,1,0:T(1,128)S(1)}, u32[]{:S(2)}, u32[]{:S(2)}) %all-to-all-start.1) | async-done | bytes 8224 | tf_op jit(solution)/shard_map/all_to_all | solution.py:98
  44.6 2.5 %fusion.5 = f32[512,256]{1,0:T(8,128)S(1)} fusion(bf16[2048,512]{1,0:T(8,128)(2,1)} %get-tuple-element.42, bf16[2048]{0:T(1024)(128)(2,1)S(1)} %get-tuple-element.18, s32[2048]{0:T(1024)S(1)} %copy-done.7), kind=kOutput, calls=%fused_computation.13 | convolution fusion | flops 537919488 | bytes 2633728 | tf_op jit(solution)/shard_map/dot_general | solution.py:108
  47.1 4.3 %multiply_convert_fusion = bf16[2048,512]{1,0:T(8,128)(2,1)S(1)} fusion(f32[2048,512]{1,0:T(8,128)} %get-tuple-element.43, bf16[2048]{0:T(1024)(128)(2,1)S(1)} %get-tuple-element.18, s32[2048]{0:T(1024)S(1)} %copy-done.7, bf16[1,512,256]{2,1,0:T(8,128)(2,1)S(1)} %copy-done.6), kind=kOutput, calls=%fused_computation.4 | convolution fusion | flops 547356672 | bytes 6565888 | tf_op jit(solution)/shard_map/dot_general | solution.py:111
  51.5 0.3 slice-done.2
  51.8 1.2 %slice-done.3 = s8[4194304]{0:T(1024)(128)(4,1)S(1)} async-done(((s8[16777216]{0:T(1024)(128)(4,1)}), s8[4194304]{0:T(1024)(128)(4,1)S(1)}, s32[]{:S(2)}) %slice-start.3) | async-done | bytes 4194328
  53.0 0.8 fusion.6
  53.8 0.8 fusion.7
  54.7 0.3 collective-permute-start
  55.0 0.8 fusion.10
  55.8 0.8 fusion.11
  56.6 0.5 collective-permute-start.3
  57.1 0.8 fusion.12
  57.9 0.8 fusion.13
  58.9 0.7 fusion.14
  59.6 0.7 fusion.24
  60.4 0.7 fusion.18
  61.1 0.8 fusion.8
  61.9 0.8 fusion.9
  62.8 0.6 collective-permute-start.1
  63.4 0.7 fusion.28
  64.1 0.7 fusion.16
  65.0 1.2 %collective-permute-start.5 = (bf16[544,256]{1,0:T(8,128)(2,1)S(1)}, bf16[544,256]{1,0:T(8,128)(2,1)S(1)}, u32[]{:S(2)}, u32[]{:S(2)}) collective-permute-start(bf16[544,256]{1,0:T(8,128)(2,1)S(1)} %get-tuple-element.24), channel_id=1, source_target_pairs={{0,6},{1,7},{2,0},{3,1},{4,2},{5,3},{6,4},{7,5},{8,14},{9,15},{10,... | collective-permute-start | bytes 835592 | tf_op jit(solution)/shard_map/ppermute | solution.py:27
  66.3 0.7 fusion.32
  67.0 0.9 collective-permute-start.8
  67.9 0.7 fusion.92
  68.6 5.1 %collective-permute-done.5 = bf16[544,256]{1,0:T(8,128)(2,1)S(1)} collective-permute-done((bf16[544,256]{1,0:T(8,128)(2,1)S(1)}, bf16[544,256]{1,0:T(8,128)(2,1)S(1)}, u32[]{:S(2)}, u32[]{:S(2)}) %collective-permute-start.5) | collective-permute-done | bytes 278560 | tf_op jit(solution)/shard_map/ppermute | solution.py:27
  74.0 2.5 %collective-permute-start.7 = (bf16[544,256]{1,0:T(8,128)(2,1)S(1)}, bf16[544,256]{1,0:T(8,128)(2,1)S(1)}, u32[]{:S(2)}, u32[]{:S(2)}) collective-permute-start(bf16[544,256]{1,0:T(8,128)(2,1)S(1)} %get-tuple-element.23), channel_id=1, source_target_pairs={{0,6},{1,7},{2,0},{3,1},{4,2},{5,3},{6,4},{7,5},{8,14},{9,15},{10,... | collective-permute-start | bytes 835592 | tf_op jit(solution)/shard_map/ppermute | solution.py:27
  76.4 0.3 collective-permute-done.8
  76.9 0.3 collective-permute-start.9
  77.2 0.7 fusion.20
  78.0 3.3 %collective-permute-start.6 = (bf16[544,256]{1,0:T(8,128)(2,1)S(1)}, bf16[544,256]{1,0:T(8,128)(2,1)S(1)}, u32[]{:S(2)}, u32[]{:S(2)}) collective-permute-start(bf16[544,256]{1,0:T(8,128)(2,1)S(1)} %get-tuple-element.22), channel_id=1, source_target_pairs={{0,6},{1,7},{2,0},{3,1},{4,2},{5,3},{6,4},{7,5},{8,14},{9,15},{10,... | collective-permute-start | bytes 835592 | tf_op jit(solution)/shard_map/ppermute | solution.py:27
  81.2 2.3 %collective-permute-done.7 = bf16[544,256]{1,0:T(8,128)(2,1)S(1)} collective-permute-done((bf16[544,256]{1,0:T(8,128)(2,1)S(1)}, bf16[544,256]{1,0:T(8,128)(2,1)S(1)}, u32[]{:S(2)}, u32[]{:S(2)}) %collective-permute-start.7) | collective-permute-done | bytes 278560 | tf_op jit(solution)/shard_map/ppermute | solution.py:27
  83.5 4.4 %collective-permute-done.9 = bf16[544,256]{1,0:T(8,128)(2,1)S(1)} collective-permute-done((bf16[544,256]{1,0:T(8,128)(2,1)S(1)}, bf16[544,256]{1,0:T(8,128)(2,1)S(1)}, u32[]{:S(2)}, u32[]{:S(2)}) %collective-permute-start.9) | collective-permute-done | bytes 278560 | tf_op jit(solution)/shard_map/ppermute | solution.py:27
  88.1 1.5 %collective-permute-start.10 = (bf16[544,256]{1,0:T(8,128)(2,1)S(1)}, bf16[544,256]{1,0:T(8,128)(2,1)S(1)}, u32[]{:S(2)}, u32[]{:S(2)}) collective-permute-start(bf16[544,256]{1,0:T(8,128)(2,1)S(1)} %fusion.53), channel_id=1, source_target_pairs={{0,8},{1,9},{2,10},{3,11},{4,12},{5,13},{6,14},{7,15},{8,0},{9,1},... | collective-permute-start | bytes 835592 | tf_op jit(solution)/shard_map/ppermute | solution.py:27
  89.6 0.7 fusion.36
  90.4 1.5 %collective-permute-done.2 = bf16[544,256]{1,0:T(8,128)(2,1)S(1)} collective-permute-done((bf16[544,256]{1,0:T(8,128)(2,1)S(1)}, bf16[544,256]{1,0:T(8,128)(2,1)S(1)}, u32[]{:S(2)}, u32[]{:S(2)}) %collective-permute-start.2) | collective-permute-done | bytes 278560 | tf_op jit(solution)/shard_map/ppermute | solution.py:27
  91.9 4.3 %collective-permute-done.10 = bf16[544,256]{1,0:T(8,128)(2,1)S(1)} collective-permute-done((bf16[544,256]{1,0:T(8,128)(2,1)S(1)}, bf16[544,256]{1,0:T(8,128)(2,1)S(1)}, u32[]{:S(2)}, u32[]{:S(2)}) %collective-permute-start.10) | collective-permute-done | bytes 278560 | tf_op jit(solution)/shard_map/ppermute | solution.py:27
  96.4 0.6 slice_bitcast_fusion.9
  97.0 1.0 %copy.20 = f32[1,256,512]{2,1,0:T(8,128)} copy(f32[1,256,512]{1,2,0:T(8,128)S(1)} %slice_bitcast_fusion) | data formatting | bytes 1048576
  (46 shorter events, 1.6 us)
Async XLA Ops:
  0.6 1.6 %copy-start = (bf16[256,4096]{1,0:T(8,128)(2,1)S(1)}, bf16[256,4096]{1,0:T(8,128)(2,1)}, u32[]{:S(2)}) copy-start(bf16[256,4096]{1,0:T(8,128)(2,1)} %param.11) | copy-start | bytes 6291460
  6.6 22.3 %all-to-all-start = ((f32[8,1,256]{2,1,0:T(1,128)}), f32[8,1,256]{2,1,0:T(1,128)S(1)}, u32[]{:S(2)}, u32[]{:S(2)}) async-start(f32[8,1,256]{2,1,0:T(1,128)} %broadcast_in_dim.39), calls=%async_computation | async-start | bytes 16384 | tf_op jit(solution)/shard_map/all_to_all | solution.py:66
  13.0 15.9 %copy-start.2 = (s32[1,16,128]{2,1,0:T(8,128)S(1)}, s32[1,16,128]{2,1,0:T(8,128)}, u32[]{:S(2)}) copy-start(s32[1,16,128]{2,1,0:T(8,128)} %param.12) | copy-start | bytes 24580
  13.0 24.0 %copy-start.6 = (bf16[1,512,256]{2,1,0:T(8,128)(2,1)S(1)}, bf16[1,512,256]{2,1,0:T(8,128)(2,1)}, u32[]{:S(2)}) copy-start(bf16[1,512,256]{2,1,0:T(8,128)(2,1)} %param.19) | copy-start | bytes 786436
  13.1 24.0 %copy-start.7 = (s32[2048]{0:T(1024)S(1)}, s32[2048]{0:T(1024)}, u32[]{:S(2)}) copy-start(s32[2048]{0:T(1024)} %param.14) | copy-start | bytes 24580
  30.3 14.3 %all-to-all-start.1 = ((f32[16,1,128]{2,1,0:T(1,128)}), f32[16,1,128]{2,1,0:T(1,128)S(1)}, u32[]{:S(2)}, u32[]{:S(2)}) async-start(f32[16,1,128]{2,1,0:T(1,128)} %bitcast.5), calls=%async_computation.1 | async-start | bytes 16384 | tf_op jit(solution)/shard_map/all_to_all | solution.py:98
  37.0 2.5 %copy-start.1 = (s32[16,16]{1,0:T(8,128)S(1)}, s32[16,16]{1,0:T(8,128)}, u32[]{:S(2)}) copy-start(s32[16,16]{1,0:T(8,128)} %param.13) | copy-start | bytes 3076
  37.0 7.5 %copy-start.3 = (f32[2048]{0:T(1024)S(1)}, f32[2048]{0:T(1024)}, u32[]{:S(2)}) copy-start(f32[2048]{0:T(1024)} %param.15) | copy-start | bytes 24580
  37.1 7.5 %copy-start.4 = (f32[2048]{0:T(1024)S(1)}, f32[2048]{0:T(1024)}, u32[]{:S(2)}) copy-start(f32[2048]{0:T(1024)} %param.17) | copy-start | bytes 24580
  37.1 7.5 %copy-start.5 = (s32[2048]{0:T(1024)S(1)}, s32[2048]{0:T(1024)}, u32[]{:S(2)}) copy-start(s32[2048]{0:T(1024)} %param.16) | copy-start | bytes 24580
  44.6 6.9 %slice-start = ((s8[16777216]{0:T(1024)(128)(4,1)}), s8[4194304]{0:T(1024)(128)(4,1)S(1)}, s32[]{:S(2)}) async-start(s8[16777216]{0:T(1024)(128)(4,1)} %bitcast.127), calls=%async_computation.2 | async-start | bytes 8388608
  47.1 4.4 %slice-start.1 = ((s8[16777216]{0:T(1024)(128)(4,1)}), s8[4194304]{0:T(1024)(128)(4,1)S(1)}, s32[]{:S(2)}) async-start(s8[16777216]{0:T(1024)(128)(4,1)} %bitcast.127), calls=%async_computation.3 | async-start | bytes 8388608
  47.1 4.7 %slice-start.2 = ((s8[16777216]{0:T(1024)(128)(4,1)}), s8[4194304]{0:T(1024)(128)(4,1)S(1)}, s32[]{:S(2)}) async-start(s8[16777216]{0:T(1024)(128)(4,1)} %bitcast.127), calls=%async_computation.4 | async-start | bytes 8388608
  47.1 5.9 %slice-start.3 = ((s8[16777216]{0:T(1024)(128)(4,1)}), s8[4194304]{0:T(1024)(128)(4,1)S(1)}, s32[]{:S(2)}) async-start(s8[16777216]{0:T(1024)(128)(4,1)} %bitcast.127), calls=%async_computation.5 | async-start | bytes 8388608
  54.7 26.5 %collective-permute-start = (bf16[2,544,256]{2,1,0:T(8,128)(2,1)S(1)}, bf16[2,544,256]{2,1,0:T(8,128)(2,1)S(1)}, u32[]{:S(2)}, u32[]{:S(2)}) collective-permute-start(bf16[2,544,256]{2,1,0:T(8,128)(2,1)S(1)} %maximum_maximum_fusion), channel_id=1, source_target_pairs={{0,1},{1,0},{2,3},{3,2},{4,5},{5,4},{6,7},{7,6},{8,9},{9,8},{10,11... | collective-permute-start | bytes 1671176 | tf_op jit(solution)/shard_map/ppermute | solution.py:27
  56.6 12.0 %collective-permute-start.3 = (bf16[2,544,256]{2,1,0:T(8,128)(2,1)S(1)}, bf16[2,544,256]{2,1,0:T(8,128)(2,1)S(1)}, u32[]{:S(2)}, u32[]{:S(2)}) collective-permute-start(bf16[2,544,256]{2,1,0:T(8,128)(2,1)S(1)} %maximum_maximum_fusion.2), channel_id=1, source_target_pairs={{0,1},{1,0},{2,3},{3,2},{4,5},{5,4},{6,7},{7,6},{8,9},{9,8},{10,11... | collective-permute-start | bytes 1671176 | tf_op jit(solution)/shard_map/ppermute | solution.py:27
  58.8 6.1 %collective-permute-start.4 = (bf16[2,544,256]{2,1,0:T(8,128)(2,1)S(1)}, bf16[2,544,256]{2,1,0:T(8,128)(2,1)S(1)}, u32[]{:S(2)}, u32[]{:S(2)}) collective-permute-start(bf16[2,544,256]{2,1,0:T(8,128)(2,1)S(1)} %maximum_maximum_fusion.3), channel_id=1, source_target_pairs={{0,1},{1,0},{2,3},{3,2},{4,5},{5,4},{6,7},{7,6},{8,9},{9,8},{10,11... | collective-permute-start | bytes 1671176 | tf_op jit(solution)/shard_map/ppermute | solution.py:27
  62.8 13.6 %collective-permute-start.1 = (bf16[2,544,256]{2,1,0:T(8,128)(2,1)S(1)}, bf16[2,544,256]{2,1,0:T(8,128)(2,1)S(1)}, u32[]{:S(2)}, u32[]{:S(2)}) collective-permute-start(bf16[2,544,256]{2,1,0:T(8,128)(2,1)S(1)} %maximum_maximum_fusion.1), channel_id=1, source_target_pairs={{0,1},{1,0},{2,3},{3,2},{4,5},{5,4},{6,7},{7,6},{8,9},{9,8},{10,11... | collective-permute-start | bytes 1671176 | tf_op jit(solution)/shard_map/ppermute | solution.py:27
  65.0 8.7 %collective-permute-start.5 = (bf16[544,256]{1,0:T(8,128)(2,1)S(1)}, bf16[544,256]{1,0:T(8,128)(2,1)S(1)}, u32[]{:S(2)}, u32[]{:S(2)}) collective-permute-start(bf16[544,256]{1,0:T(8,128)(2,1)S(1)} %get-tuple-element.24), channel_id=1, source_target_pairs={{0,6},{1,7},{2,0},{3,1},{4,2},{5,3},{6,4},{7,5},{8,14},{9,15},{10,... | collective-permute-start | bytes 835592 | tf_op jit(solution)/shard_map/ppermute | solution.py:27
  67.0 9.7 %collective-permute-start.8 = (bf16[544,256]{1,0:T(8,128)(2,1)S(1)}, bf16[544,256]{1,0:T(8,128)(2,1)S(1)}, u32[]{:S(2)}, u32[]{:S(2)}) collective-permute-start(bf16[544,256]{1,0:T(8,128)(2,1)S(1)} %get-tuple-element.25), channel_id=1, source_target_pairs={{0,2},{1,3},{2,4},{3,5},{4,6},{5,7},{6,0},{7,1},{8,10},{9,11},{10,... | collective-permute-start | bytes 835592 | tf_op jit(solution)/shard_map/ppermute | solution.py:27
  74.0 9.6 %collective-permute-start.7 = (bf16[544,256]{1,0:T(8,128)(2,1)S(1)}, bf16[544,256]{1,0:T(8,128)(2,1)S(1)}, u32[]{:S(2)}, u32[]{:S(2)}) collective-permute-start(bf16[544,256]{1,0:T(8,128)(2,1)S(1)} %get-tuple-element.23), channel_id=1, source_target_pairs={{0,6},{1,7},{2,0},{3,1},{4,2},{5,3},{6,4},{7,5},{8,14},{9,15},{10,... | collective-permute-start | bytes 835592 | tf_op jit(solution)/shard_map/ppermute | solution.py:27
  76.9 11.0 %collective-permute-start.9 = (bf16[544,256]{1,0:T(8,128)(2,1)S(1)}, bf16[544,256]{1,0:T(8,128)(2,1)S(1)}, u32[]{:S(2)}, u32[]{:S(2)}) collective-permute-start(bf16[544,256]{1,0:T(8,128)(2,1)S(1)} %get-tuple-element.21), channel_id=1, source_target_pairs={{0,2},{1,3},{2,4},{3,5},{4,6},{5,7},{6,0},{7,1},{8,10},{9,11},{10,... | collective-permute-start | bytes 835592 | tf_op jit(solution)/shard_map/ppermute | solution.py:27
  78.0 12.4 %collective-permute-start.6 = (bf16[544,256]{1,0:T(8,128)(2,1)S(1)}, bf16[544,256]{1,0:T(8,128)(2,1)S(1)}, u32[]{:S(2)}, u32[]{:S(2)}) collective-permute-start(bf16[544,256]{1,0:T(8,128)(2,1)S(1)} %get-tuple-element.22), channel_id=1, source_target_pairs={{0,6},{1,7},{2,0},{3,1},{4,2},{5,3},{6,4},{7,5},{8,14},{9,15},{10,... | collective-permute-start | bytes 835592 | tf_op jit(solution)/shard_map/ppermute | solution.py:27
  81.2 10.7 %collective-permute-start.2 = (bf16[544,256]{1,0:T(8,128)(2,1)S(1)}, bf16[544,256]{1,0:T(8,128)(2,1)S(1)}, u32[]{:S(2)}, u32[]{:S(2)}) collective-permute-start(bf16[544,256]{1,0:T(8,128)(2,1)S(1)} %get-tuple-element.20), channel_id=1, source_target_pairs={{0,2},{1,3},{2,4},{3,5},{4,6},{5,7},{6,0},{7,1},{8,10},{9,11},{10,... | collective-permute-start | bytes 835592 | tf_op jit(solution)/shard_map/ppermute | solution.py:27
  88.1 8.1 %collective-permute-start.10 = (bf16[544,256]{1,0:T(8,128)(2,1)S(1)}, bf16[544,256]{1,0:T(8,128)(2,1)S(1)}, u32[]{:S(2)}, u32[]{:S(2)}) collective-permute-start(bf16[544,256]{1,0:T(8,128)(2,1)S(1)} %fusion.53), channel_id=1, source_target_pairs={{0,8},{1,9},{2,10},{3,11},{4,12},{5,13},{6,14},{7,15},{8,0},{9,1},... | collective-permute-start | bytes 835592 | tf_op jit(solution)/shard_map/ppermute | solution.py:27
